TPU v7x, 128 devices: a whole 4x4x4 slice. The times are simulated.
128 devices in a mesh: req: 16 (over x, z), exp: 8 (over y, core).
Axes of the slice: x: 4, y: 4, z: 4, core: 2. Of those that a mesh axis runs over, the one named last changes fastest.
Arguments:
- tokens: bfloat16 [16384, 2048], P('req'), may hold values from -40 to 40
- routes: int32 [16384, 2], P('req'), may hold values from 0 to 7, all different within a row; in each aligned block of 1024 rows (0 to 1023, 1024 to 2047, ...) at most 320 rows name the same one
- lengths: int32 [64], P('req'), may hold values from 1 to 256, 8192 in all
- cached_prefix_length: int32 [64], P('req'), may hold values from 0 to 64, as said below
- prefix_cache_row: int32 [64], replicated, may hold values from 0 to 15, as said below
- adapter_per_request: int32 [64], P('req'), may hold values from 0 to 63
- adapter_storage_slot: int32 [64], replicated, may hold values from 0 to 63, each once
- router_weight: bfloat16 [2048, 8], replicated, may hold values from -0.125 to 0.125
- key_value_weight: bfloat16 [2048, 4096], P('req', 'exp'), may hold values from -0.125 to 0.125
- expert_query_weight: bfloat16 [2048, 8, 2048], P('req', None, 'exp'), may hold values from -0.125 to 0.125
- expert_output_weight: bfloat16 [8, 2048, 2048], P(None, 'exp', 'req'), may hold values from -0.125 to 0.125
- adapter_down_maps: bfloat16 [64, 2048, 16], P('req'), may hold values from -0.125 to 0.125
- adapter_up_maps: bfloat16 [64, 16, 4096], P('req', None, 'exp'), may hold values from -1.5 to 1.5
- prefix_cache_store: bfloat16 [64, 64, 4096], P('req', None, 'exp'), may hold values from -6 to 6
Outputs:
- attention_out: bfloat16 [16384, 2048], P('req', 'exp')
Inputs may be any that keep to these rules, and one draw needn't show every extreme that they name: `routes`: in each aligned block of 1024 rows (one group) no expert is named by more than 320 rows, and one is named by exactly 320. The lengths sum to 8192 and some request has exactly 256. `cached_prefix_length`: exactly 32 requests have no cached prefix; some request has exactly 64. `prefix_cache_row`: request j of a group keeps its cache in slot j of its row; each row holds exactly one cache in each slot, and no row holds two caches of one group. `adapter_storage_slot`: each slot holds one adapter.
All inputs are finite; a program needn't handle non-finite values. No bound on the sum of `lengths` on one device may be relied on, other than what follows from the above.
Results may differ from a plain program's by a relative error of at most 0.017.
The roundings to bfloat16 on the way count: a program that leaves them out, or rounds other values in their place, can miss the bound.
Values may be sent and summed in bfloat16 or wider, within the bound.
No kernel may reach another device: no remote copies, remote signals or barrier semaphores. Data moves between devices by JAX's collectives and lax.ppermute only.
A program may use at most 128 MiB of HBM per device.

v0:
```python
import jax
import jax.numpy as jnp
from jax import lax
from jax.sharding import PartitionSpec as P

HD = 128
NE = 8
TOPK = 2
CAP = 320
adapter_scale = 0.5


def compact(routes):
    route_flat = routes.reshape(-1)
    pair_count = route_flat.shape[0]
    one_hot = (route_flat[:, None] == jnp.arange(NE, dtype=jnp.int32)[None, :]).astype(jnp.int32)
    earlier = jnp.cumsum(one_hot, axis=0) - one_hot
    route_rank = jnp.sum(earlier * one_hot, axis=1)
    slot_table = (
        jnp.zeros((NE, CAP), jnp.int32)
        .at[route_flat, route_rank]
        .set(jnp.arange(pair_count, dtype=jnp.int32))
    )
    return (route_flat, route_rank, slot_table)


def attend(queries, all_keys, cached_prefix_length):
    per_request = queries.shape[1]
    key_span = all_keys.shape[1]
    cached = key_span - per_request
    scores = jnp.einsum(
        "rtjhd,rshd->rhtjs", queries, all_keys[:, :, :, 0, :], preferred_element_type=jnp.float32
    ) * queries.shape[-1] ** (-0.5)
    key_place = jnp.arange(key_span, dtype=jnp.int32)
    query_place = jnp.arange(per_request, dtype=jnp.int32)
    from_cache = key_place[None, :] < cached_prefix_length[:, None]
    from_prompt = (key_place[None, :] >= cached) & (
        key_place[None, :] - cached <= query_place[:, None]
    )
    allowed = jnp.where(
        key_place[None, None, :] < cached, from_cache[:, None, :], from_prompt[None, :, :]
    )
    allowed = allowed[:, None, :, None, :]
    row_max = jnp.max(jnp.where(allowed, scores, -jnp.inf), axis=-1, keepdims=True)
    weights = jnp.where(allowed, jnp.exp(scores - row_max), 0.0)
    probability = (weights / jnp.sum(weights, axis=-1, keepdims=True)).astype(jnp.bfloat16)
    return jnp.einsum(
        "rhtjs,rshd->rtjhd",
        probability,
        all_keys[:, :, :, 1, :],
        preferred_element_type=jnp.float32,
    ).astype(jnp.bfloat16)


def body(
    tokens,
    routes,
    lengths,
    cached_prefix_length,
    prefix_cache_row,
    adapter_per_request,
    adapter_storage_slot,
    router_weight,
    key_value_weight,
    expert_query_weight,
    expert_output_weight,
    adapter_down_maps,
    adapter_up_maps,
    prefix_cache_store,
):
    group_index = lax.axis_index("req")
    num_requests = lengths.shape[0]
    tok_rows = tokens.shape[0]
    per_request = tok_rows // num_requests
    model_width = tokens.shape[1]
    kv_cols = key_value_weight.shape[1]
    query_cols = expert_query_weight.shape[2]
    heads = kv_cols // (2 * HD)
    cached = prefix_cache_store.shape[1]
    route_flat, route_rank, slot_table = compact(routes)
    picked = tokens[slot_table // 2]
    pieces = (
        lax.all_gather(key_value_weight, "req", axis=0, tiled=True),
        lax.all_gather(expert_query_weight, "req", axis=0, tiled=True),
    )
    key_value_segment = jnp.dot(tokens, pieces[0], preferred_element_type=jnp.float32)
    query_run = jnp.einsum("kcd,dkh->kch", picked, pieces[1], preferred_element_type=jnp.float32)
    adapter_hot = (
        adapter_per_request[:, None]
        == jnp.arange(adapter_storage_slot.shape[0], dtype=jnp.int32)[None, :]
    ).astype(jnp.int32)
    wanted = jnp.sum(adapter_hot * adapter_storage_slot[None, :], axis=1)
    pieces = (
        lax.all_gather(adapter_down_maps, "req", axis=0, tiled=True),
        lax.all_gather(adapter_up_maps, "req", axis=0, tiled=True),
    )
    row_count = pieces[0].shape[0]
    matches = (wanted[:, None] == jnp.arange(row_count, dtype=jnp.int32)[None, :]).astype(
        jnp.bfloat16
    )
    down_run = jnp.einsum("rn,ndq->rdq", matches, pieces[0], preferred_element_type=jnp.float32)
    up_run = jnp.einsum("rn,nqc->rqc", matches, pieces[1], preferred_element_type=jnp.float32)
    reduced_rank_state = jnp.einsum(
        "rtd,rdq->rtq",
        tokens.reshape(num_requests, per_request, model_width),
        down_run.astype(jnp.bfloat16),
        preferred_element_type=jnp.float32,
    ).astype(jnp.bfloat16)
    adapter_term = jnp.einsum(
        "mdg,mgy->mdy",
        reduced_rank_state,
        up_run.astype(jnp.bfloat16),
        preferred_element_type=jnp.float32,
    ).reshape(tok_rows, kv_cols)
    fresh_key_value = (key_value_segment + adapter_scale * adapter_term).astype(jnp.bfloat16)
    own_rows = lax.dynamic_slice_in_dim(
        prefix_cache_row, group_index * num_requests, num_requests, 0
    )
    wanted_slot = own_rows * num_requests + jnp.arange(num_requests, dtype=jnp.int32)
    shard_piece = lax.all_gather(prefix_cache_store, "req", axis=0, tiled=True)
    row_count = shard_piece.shape[0]
    matches = (wanted_slot[:, None] == jnp.arange(row_count, dtype=jnp.int32)[None, :]).astype(
        jnp.bfloat16
    )
    stored = jnp.einsum(
        "rn,nsc->rsc", matches, shard_piece, preferred_element_type=jnp.float32
    ).astype(jnp.bfloat16)
    all_keys = jnp.concatenate(
        [stored, fresh_key_value.reshape(num_requests, per_request, kv_cols)], axis=1
    )
    all_keys = all_keys.reshape(num_requests, cached + per_request, heads, 2, HD)
    queries = query_run.astype(jnp.bfloat16)[route_flat, route_rank].reshape(
        num_requests, per_request, TOPK, heads, HD
    )
    attended = attend(queries, all_keys, cached_prefix_length)
    gathered = attended.reshape(TOPK * tok_rows, query_cols)[slot_table]
    logits = jnp.dot(tokens, router_weight, preferred_element_type=jnp.float32)
    route_hot = (routes[:, :, None] == jnp.arange(NE, dtype=jnp.int32)[None, None, :]).astype(
        jnp.float32
    )
    chosen = jnp.sum(route_hot * logits[:, None, :], axis=-1)
    gate_values = jax.nn.sigmoid(chosen - chosen[:, ::-1])
    live_rows = (
        (jnp.arange(per_request, dtype=jnp.int32)[None, :] < lengths[:, None])
        .reshape(tok_rows)
        .astype(jnp.float32)
    )
    shard_piece = lax.all_gather(expert_output_weight, "req", axis=2, tiled=True)
    out_blocks = jnp.einsum(
        "kch,khn->kcn", gathered, shard_piece, preferred_element_type=jnp.float32
    )
    per_pair = out_blocks[route_flat, route_rank].reshape(tok_rows, TOPK, shard_piece.shape[2])
    partial_value = jnp.sum(per_pair * gate_values[:, :, None], axis=1) * live_rows[:, None]
    return lax.psum_scatter(
        partial_value.astype(jnp.bfloat16), "exp", scatter_dimension=1, tiled=True
    )


def solution(mesh):
    return jax.shard_map(
        body,
        mesh=mesh,
        in_specs=(
            P("req", None),
            P("req", None),
            P("req"),
            P("req"),
            P(),
            P("req"),
            P(),
            P(),
            P("req", "exp"),
            P("req", None, "exp"),
            P(None, "exp", "req"),
            P("req", None, None),
            P("req", None, "exp"),
            P("req", None, "exp"),
        ),
        out_specs=P("req", "exp"),
        check_vma=False,
    )
```

profile of v0, /device:TPU:0, one launch (start us, length us, event | category | flops | bytes accessed | tf_op | source)
XLA Modules:
  0.0 522.8 jit_solution(609906091671764247)
XLA Ops:
  6.5 0.7 all-gather.13.cloned.1.call-update
  7.3 0.7 all-gather.7.cloned.1.call-update
  9.4 1.9 copy.58
  12.0 0.9 copy.55
  13.8 2.3 reduce-window.6
  16.9 8.1 %scatter_custom_fusion = s32[2560]{0:T(1024)S(1)} fusion(s32[2048]{0:T(1024)S(1)} %broadcast_select_fusion.1, s32[2048]{0:T(1024)S(1)} %iota.56, s32[]{:T(128)} %constant.20.clone.1), kind=kCustom, calls=%fused_computation.75 | custom fusion | bytes 10244
  25.3 22.9 %gather_fusion = bf16[2560,2048]{1,0:T(8,128)(2,1)} fusion(bf16[1024,2048]{1,0:T(8,128)(2,1)} %param.14, s32[3072]{0:T(1024)S(1)} %pad_clamp_fusion.1), kind=kCustom, calls=%fused_computation | custom fusion | bytes 20981760 | tf_op jit(solution)/shard_map/gather | solution.py:81
  48.2 3.4 fusion.60
  53.3 1.6 all-gather.13.cloned.1.call-done
  54.8 3.0 convolution_convert_fusion.1
  57.9 50.1 %all-gather.7.cloned.1.call-done = bf16[64,64,512]{2,1,0:T(8,128)(2,1)} async-done(((bf16[4,64,512]{2,1,0:T(8,128)(2,1)}), bf16[64,64,512]{2,1,0:T(8,128)(2,1)}) %all-gather.7.cloned.1.call-update) | async-done | bytes 4194320 | tf_op jit(solution)/shard_map/all_gather | solution.py:120
  107.9 6.7 %fusion.21 = bf16[4,64,512]{2,0,1:T(4,128)(2,1)S(1)} fusion(bf16[64,64,512]{2,1,0:T(8,128)(2,1)} %all-gather.7.cloned.1.call-done, s32[4]{0:T(128)S(1)} %iota_add_fusion.1), kind=kOutput, calls=%fused_computation.29 | convolution fusion | flops 16908544 | bytes 4456464 | tf_op jit(solution)/shard_map/rn,nsc->rsc/dot_general | solution.py:125
  114.8 46.6 %all-gather.11.cloned.1.call-done = bf16[64,2048,16]{1,2,0:T(8,128)(2,1)} async-done(((bf16[4,2048,16]{1,2,0:T(8,128)(2,1)}), bf16[64,2048,16]{1,2,0:T(8,128)(2,1)}) %all-gather.11.cloned.1.call-update) | async-done | bytes 4194320 | tf_op jit(solution)/shard_map/all_gather | solution.py:94
  161.4 6.7 %fusion.15 = bf16[4,2048,16]{1,0,2:T(4,128)(2,1)S(1)} fusion(bf16[64,2048,16]{1,2,0:T(8,128)(2,1)} %all-gather.11.cloned.1.call-done, s32[4]{0:T(128)S(1)} %select_reduce_fusion.2), kind=kOutput, calls=%fused_computation.22 | convolution fusion | flops 16908544 | bytes 4456464 | tf_op jit(solution)/shard_map/rn,ndq->rdq/dot_general | solution.py:101
  168.1 4.0 convolution_multiply_fusion
  172.0 36.2 %all-gather.9.cloned.1.call-done = bf16[2048,512]{1,0:T(8,128)(2,1)} async-done(((bf16[128,512]{1,0:T(8,128)(2,1)}), bf16[2048,512]{1,0:T(8,128)(2,1)}) %all-gather.9.cloned.1.call-update) | async-done | bytes 2097168 | tf_op jit(solution)/shard_map/all_gather | solution.py:83
  208.2 6.2 %fusion.18 = bf16[1024,512]{1,0:T(8,128)(2,1)} fusion(f32[4,256,512]{2,1,0:T(8,128)S(1)} %convolution_multiply_fusion, bf16[1024,2048]{1,0:T(8,128)(2,1)} %param.14, bf16[2048,512]{1,0:T(8,128)(2,1)} %all-gather.9.cloned.1.call-done), kind=kOutput, calls=%fused_computation.24 | convolution fusion | flops 2148532224 | bytes 9437184 | tf_op jit(solution)/shard_map/dot_general | solution.py:86
  214.5 1.3 concatenate.14
  216.2 64.2 %all-gather.15.cloned.1.call-done = bf16[2048,8,256]{2,0,1:T(8,128)(2,1)} async-done(((bf16[128,8,256]{2,0,1:T(8,128)(2,1)}), bf16[2048,8,256]{2,0,1:T(8,128)(2,1)}) %all-gather.15.cloned.1.call-update) | async-done | bytes 8388624 | tf_op jit(solution)/shard_map/all_gather | solution.py:84
  280.4 9.2 %convolution_convert_fusion = bf16[8,320,256]{2,1,0:T(8,128)(2,1)S(1)} fusion(bf16[8,320,2048]{2,1,0:T(8,128)(2,1)} %bitcast.79, bf16[2048,8,256]{2,0,1:T(8,128)(2,1)} %all-gather.15.cloned.1.call-done), kind=kOutput, calls=%fused_computation.26 | convolution fusion | flops 2685009920 | bytes 20185088 | tf_op jit(solution)/shard_map/kcd,dkh->kch/dot_general | solution.py:87
  289.7 11.1 %gather_fusion.1 = bf16[2048,256]{1,0:T(8,128)(2,1)S(1)} fusion(bf16[8,320,256]{2,1,0:T(8,128)(2,1)S(1)} %convolution_convert_fusion, s32[2048]{0:T(1024)S(1)} %bitcast.76), kind=kCustom, calls=%fused_computation.1 | custom fusion | bytes 2113536 | tf_op jit(solution)/shard_map/gather | solution.py:132
  301.1 6.3 %fusion.54 = (f32[4,2,256,2]{2,3,1,0:T(2,128)S(1)}, f32[4,2,256,2,320]{2,4,3,1,0:T(8,128)}) fusion(pred[4,256,320]{1,2,0:T(8,128)(4,1)S(1)} %broadcast_select_fusion, bf16[4,256,2,2,128]{4,3,2,1,0:T(2,128)(2,1)S(1)} %reshape.178, bf16[4,320,2,2,128]{4,1,2,0,3:T(8,128)(2,1)} %copy-done.2), kind=kOutput, calls=%fused_computation.96 | convolution fusion | flops 678953280 | bytes 9322496 | tf_op jit(solution)/shard_map/sub | solution.py:45
  307.4 3.3 fusion.20
  310.6 0.8 copy.60
  311.6 7.6 %gather_fusion.2 = bf16[2560,256]{1,0:T(8,128)(2,1)S(1)} fusion(bf16[2048,256]{1,0:T(8,128)(2,1)S(1)} %bitcast.78, s32[3072]{0:T(1024)S(1)} %pad_clamp_fusion), kind=kCustom, calls=%fused_computation.2 | custom fusion | bytes 2631680 | tf_op jit(solution)/shard_map/gather | solution.py:136
  319.2 41.3 %all-gather.17.cloned.1.call-done = bf16[8,256,2048]{2,1,0:T(8,128)(2,1)} async-done(((bf16[8,256,128]{2,1,0:T(8,128)(2,1)}), bf16[8,256,2048]{2,1,0:T(8,128)(2,1)}) %all-gather.17.cloned.1.call-update) | async-done | bytes 8388624 | tf_op jit(solution)/shard_map/all_gather | solution.py:148
  360.5 12.0 %fusion.59 = f32[8,320,2048]{2,1,0:T(8,128)} fusion(bf16[8,320,256]{2,1,0:T(8,128)(2,1)S(1)} %bitcast.80, bf16[8,256,2048]{2,1,0:T(8,128)(2,1)} %all-gather.17.cloned.1.call-done), kind=kOutput, calls=%fused_computation.97 | convolution fusion | flops 2684354560 | bytes 30670848 | tf_op jit(solution)/shard_map/kch,khn->kcn/dot_general | solution.py:149
  372.5 51.1 %gather_fusion.3 = f32[2048,2048]{1,0:T(8,128)} fusion(f32[8,320,2048]{2,1,0:T(8,128)} %fusion.59, s32[2048]{0:T(1024)S(1)} %bitcast.77), kind=kCustom, calls=%fused_computation.3 | custom fusion | bytes 33570816 | tf_op jit(solution)/shard_map/gather | solution.py:152
  423.6 20.0 %reshape.180 = f32[1024,2,2048]{2,1,0:T(2,128)} reshape(f32[2048,2048]{1,0:T(8,128)} %gather_fusion.3) | data formatting | bytes 33554432 | tf_op jit(solution)/shard_map/reshape | solution.py:152
  443.6 29.1 %multiply_reduce_fusion = f32[1024,2048]{1,0:T(8,128)} fusion(f32[1024,2,2048]{2,1,0:T(2,128)} %reshape.180, f32[1024,2]{1,0:T(8,128)S(1)} %copy.61), kind=kLoop, calls=%fused_computation.6 | loop fusion | flops 6291456 | bytes 25174016 | tf_op jit(solution)/shard_map/reduce_sum | solution.py:153
  472.8 5.8 %multiply_convert_fusion = bf16[1024,2048]{1,0:T(8,128)(2,1)} fusion(f32[1024,2048]{1,0:T(8,128)} %multiply_reduce_fusion, f32[1024]{0:T(1024)S(1)} %bitcast.83), kind=kLoop, calls=%fused_computation.7 | loop fusion | flops 4194304 | bytes 12587008 | tf_op jit(solution)/shard_map/convert_element_type | solution.py:155
  478.6 37.3 %reduce-scatter.2.cloned.1.call-done = bf16[1024,256]{1,0:T(8,128)(2,1)} async-done(((bf16[1024,2048]{1,0:T(8,128)(2,1)}), bf16[1024,256]{1,0:T(8,128)(2,1)}) %reduce-scatter.2.cloned.1.call-update) | async-done | bytes 524304 | tf_op jit(solution)/shard_map/reduce_scatter | solution.py:154
  (74 shorter events, 6.5 us)
Async XLA Ops:
  6.5 41.6 %copy-start = (bf16[2048,8]{0,1:T(8,128)(2,1)S(1)}, bf16[2048,8]{0,1:T(8,128)(2,1)}, u32[]{:S(2)}) copy-start(bf16[2048,8]{0,1:T(8,128)(2,1)} %param.21) | copy-start | bytes 98308
  6.5 10.2 %copy-start.7 = (s32[2]{0:T(128)S(1)}, s32[2]{0:T(128)}, u32[]{:S(2)}) copy-start(s32[2]{0:T(128)} %constant.62) | copy-start | bytes 28
  6.5 10.3 %copy-start.6 = (s32[2]{0:T(128)S(1)}, s32[2]{0:T(128)}, u32[]{:S(2)}) copy-start(s32[2]{0:T(128)} %constant.65) | copy-start | bytes 28
  6.5 48.3 %all-gather.13.cloned.1.call-start = ((), (), s32[]{:S(2)}) async-start(), calls=%async_computation.4 | async-start | bytes 1114112 | tf_op jit(solution)/shard_map/all_gather | solution.py:95
  7.3 100.7 %all-gather.7.cloned.1.call-start = ((), (), s32[]{:S(2)}) async-start(), calls=%async_computation.1 | async-start | bytes 4456448 | tf_op jit(solution)/shard_map/all_gather | solution.py:120
  8.0 153.3 %all-gather.11.cloned.1.call-start = ((), (), s32[]{:S(2)}) async-start(), calls=%async_computation.3 | async-start | bytes 4456448 | tf_op jit(solution)/shard_map/all_gather | solution.py:94
  8.7 199.5 %all-gather.9.cloned.1.call-start = ((), (), s32[]{:S(2)}) async-start(), calls=%async_computation.2 | async-start | bytes 2228224 | tf_op jit(solution)/shard_map/all_gather | solution.py:83
  9.3 271.1 %all-gather.15.cloned.1.call-start = ((), (), s32[]{:S(2)}) async-start(), calls=%async_computation.5 | async-start | bytes 8912896 | tf_op jit(solution)/shard_map/all_gather | solution.py:84
  11.3 349.2 %all-gather.17.cloned.1.call-start = ((), (), s32[]{:S(2)}) async-start(), calls=%async_computation.6 | async-start | bytes 8912896 | tf_op jit(solution)/shard_map/all_gather | solution.py:148
  11.9 504.0 %reduce-scatter.2.cloned.1.call-start = ((), (), s32[]{:S(2)}) async-start(), calls=%async_computation.7 | async-start | bytes 4718592 | tf_op jit(solution)/shard_map/reduce_scatter | solution.py:154
  48.1 3.5 copy-start.4
  48.1 4.2 copy-start.5
  48.1 4.3 copy-start.9
  48.2 4.4 copy-start.10
  48.2 4.4 copy-start.11
  48.2 4.6 copy-start.8
  216.2 64.2 %copy-start.2 = (bf16[4,320,2,2,128]{4,1,2,0,3:T(8,128)(2,1)}, bf16[4,320,2,2,128]{4,1,2,0,3:T(8,128)(2,1)S(1)}, u32[]{:S(2)}) copy-start(bf16[4,320,2,2,128]{4,1,2,0,3:T(8,128)(2,1)S(1)} %copy_dynamic-update-slice_fusion) | copy-start | bytes 3932164
  301.1 6.3 %copy-start.3 = (bf16[4,320,2,2,128]{4,1,2,0,3:T(8,128)(2,1)S(1)}, bf16[4,320,2,2,128]{4,1,2,0,3:T(8,128)(2,1)}, u32[]{:S(2)}) copy-start(bf16[4,320,2,2,128]{4,1,2,0,3:T(8,128)(2,1)} %copy-done.2) | copy-start | bytes 3932164
  472.8 43.2 %copy-start.1 = (bf16[2048,8]{0,1:T(8,128)(2,1)S(1)}, bf16[2048,8]{0,1:T(8,128)(2,1)}, u32[]{:S(2)}) copy-start(bf16[2048,8]{0,1:T(8,128)(2,1)} %param.21) | copy-start | bytes 98308
Sparse Core Ops, SparseCore 0:
  9.5 45.2 all-gather.12
  57.0 50.9 all-gather.6
  110.1 51.2 all-gather.10
  163.4 44.8 all-gather.8
  210.3 70.1 all-gather.14
  282.4 78.0 all-gather.16
  478.7 37.1 reduce-scatter.1
where the time goes:
time: 525 us; the launch traced here: 523 us
  waiting for transfers between devices  280 us (53%)
  local copies, waits for them, and re-layouts  129 us (25%)
  matrix products  60.9 us (12%)
  other arithmetic  38.7 us (7%)
  between operations  13.8 us (3%)
    all_gather x1, waiting for transfers between devices, body(): lax.all_gather(expert_query_weight, 'req', axis=0, tiled=True)  64.2 us
    gather x1, local copies, waits for them, and re-layouts, body(): out_blocks[route_flat, route_rank]  51.1 us
    all_gather x1, waiting for transfers between devices, body(): shard_piece = lax.all_gather(prefix_cache_store, 'req', axis=0, tiled=True)  50.1 us
    all_gather x1, waiting for transfers between devices, body(): lax.all_gather(adapter_down_maps, 'req', axis=0, tiled=True)  46.6 us
    all_gather x1, waiting for transfers between devices, body(): lax.all_gather(expert_output_weight, 'req', axis=2, tiled=True)  41.3 us
    reduce_scatter x1, waiting for transfers between devices, body(): lax.psum_scatter(partial_value.astype(jnp.bfloat16), 'exp', scatter_dimen...  37.3 us
    all_gather x1, waiting for transfers between devices, body(): lax.all_gather(key_value_weight, 'req', axis=0, tiled=True)  36.2 us
    reduce_sum x1, other arithmetic, body(): jnp.sum(per_pair * gate_values[:, :, None], axis=1) * live_rows[:, None]  29.1 us
  transfers between devices with their start and end apart: 7, of which 7 were waited for; matrix products, arithmetic and copies ran while one was open for 21% of the time, Pallas kernels for 0%

commit v1 on v0

--- a/solution.py
+++ b/solution.py
@@ -1,3 +1,4 @@
+import functools
 import jax
 import jax.numpy as jnp
 from jax import lax
@@ -8,6 +9,20 @@
 TOPK = 2
 CAP = 320
 adapter_scale = 0.5
+
+
+def _state_islands(u, dev_axis):
+    n_axis = jax.lax.axis_size(dev_axis)
+    before = [None] * n_axis
+    nodes = [(to_i, (to_i + 1) % n_axis) for to_i in range(n_axis)]
+    before[n_axis - 1] = u
+    for no in range(n_axis - 2, -1, -1):
+        before[no] = jax.lax.ppermute(before[no + 1], dev_axis, nodes)
+    z1 = jnp.concatenate(before, 2)
+    return jnp.roll(z1, (jax.lax.axis_index(dev_axis) + 1) * u.shape[2], 2)
+
+
+define_state = functools.partial(_state_islands, dev_axis="req")
 
 
 def compact(routes):
@@ -145,7 +160,7 @@
         .reshape(tok_rows)
         .astype(jnp.float32)
     )
-    shard_piece = lax.all_gather(expert_output_weight, "req", axis=2, tiled=True)
+    shard_piece = define_state(expert_output_weight)
     out_blocks = jnp.einsum(
         "kch,khn->kcn", gathered, shard_piece, preferred_element_type=jnp.float32
     )

time: 525 us -> 582 us (1.11); the launches traced: 523 us -> 572 us
  local copies, waits for them, and re-layouts: 129 us -> 178 us
  waiting for transfers between devices: 280 us -> 272 us
  other arithmetic: 38.7 us -> 45.3 us
    ppermute x0 -> x15, waiting for transfers between devices: none -> 230 us  [_state_islands(): before[no] = jax.lax.ppermute(before[no + 1], dev_axis, nodes)]
    all_gather x1, waiting for transfers between devices: 64.2 us -> 0.02 us  [body(): lax.all_gather(expert_query_weight, 'req', axis=0, tiled=True)]
    all_gather x1, waiting for transfers between devices: 50.1 us -> 0.01 us  [body(): shard_piece = lax.all_gather(prefix_cache_store, 'req', axis=0, tiled=True)]
    unnamed x30 -> x65, local copies, waits for them, and re-layouts: 11.2 us -> 59.6 us
    all_gather x1, waiting for transfers between devices: 46.6 us -> 0.02 us  [body(): lax.all_gather(adapter_down_maps, 'req', axis=0, tiled=True)]
    all_gather x1 -> x0, waiting for transfers between devices: 41.3 us -> none  [body(): lax.all_gather(expert_output_weight, 'req', axis=2, tiled=True)]
    all_gather x1, waiting for transfers between devices: 36.2 us -> 0.02 us  [body(): lax.all_gather(key_value_weight, 'req', axis=0, tiled=True)]
  transfers between devices with their start and end apart: 7 -> 21, of which waited for: 7 -> 15; matrix products, arithmetic and copies ran while one was open for 21% -> 22% of each run, Pallas kernels for 0% -> 0%
where the time goes in v1:
time: 582 us; the launch traced here: 572 us
  waiting for transfers between devices  272 us (47%)
  local copies, waits for them, and re-layouts  178 us (31%)
  matrix products  60.5 us (10%)
  other arithmetic  45.3 us (8%)
  between operations  14 us (2%)
    ppermute x15, waiting for transfers between devices, _state_islands(): before[no] = jax.lax.ppermute(before[no + 1], dev_axis, nodes)  230 us
    unnamed x65, local copies, waits for them, and re-layouts  59.6 us
    gather x1, local copies, waits for them, and re-layouts, body(): out_blocks[route_flat, route_rank]  51.1 us
    reduce_scatter x1, waiting for transfers between devices, body(): lax.psum_scatter(partial_value.astype(jnp.bfloat16), 'exp', scatter_dimen...  39.1 us
    reduce_sum x1, other arithmetic, body(): jnp.sum(per_pair * gate_values[:, :, None], axis=1) * live_rows[:, None]  30.3 us
    gather x1, local copies, waits for them, and re-layouts, body(): picked = tokens[slot_table // 2]  22.9 us
    reshape x1, local copies, waits for them, and re-layouts, body(): out_blocks[route_flat, route_rank]  20 us
    dot_general x1, matrix products, body(): jnp.einsum('kch,khn->kcn', gathered, shard_piece, preferred_element_type=...  12.2 us
  transfers between devices with their start and end apart: 21, of which 15 were waited for; matrix products, arithmetic and copies ran while one was open for 22% of the time, Pallas kernels for 0%

profile of v1, /device:TPU:0, one launch (start us, length us, event | category | flops | bytes accessed | tf_op | source)
XLA Modules:
  0.0 572.5 jit_solution(11988739281538291947)
XLA Ops:
  13.4 16.8 %collective-permute-done = bf16[8,256,128]{2,1,0:T(8,128)(2,1)S(1)} collective-permute-done((bf16[8,256,128]{2,1,0:T(8,128)(2,1)}, bf16[8,256,128]{2,1,0:T(8,128)(2,1)S(1)}, u32[]{:S(2)}, u32[]{:S(2)}) %collective-permute-start) | collective-permute-done | bytes 524320 | tf_op jit(solution)/shard_map/ppermute | solution.py:20
  30.3 16.5 %collective-permute-done.1 = bf16[8,256,128]{2,1,0:T(8,128)(2,1)S(1)} collective-permute-done((bf16[8,256,128]{2,1,0:T(8,128)(2,1)S(1)}, bf16[8,256,128]{2,1,0:T(8,128)(2,1)S(1)}, u32[]{:S(2)}, u32[]{:S(2)}) %collective-permute-start.1) | collective-permute-done | bytes 524320 | tf_op jit(solution)/shard_map/ppermute | solution.py:20
  46.8 19.6 %collective-permute-done.2 = bf16[8,256,128]{2,1,0:T(8,128)(2,1)S(1)} collective-permute-done((bf16[8,256,128]{2,1,0:T(8,128)(2,1)S(1)}, bf16[8,256,128]{2,1,0:T(8,128)(2,1)S(1)}, u32[]{:S(2)}, u32[]{:S(2)}) %collective-permute-start.2) | collective-permute-done | bytes 524320 | tf_op jit(solution)/shard_map/ppermute | solution.py:20
  66.4 13.5 %collective-permute-done.3 = bf16[8,256,128]{2,1,0:T(8,128)(2,1)S(1)} collective-permute-done((bf16[8,256,128]{2,1,0:T(8,128)(2,1)S(1)}, bf16[8,256,128]{2,1,0:T(8,128)(2,1)S(1)}, u32[]{:S(2)}, u32[]{:S(2)}) %collective-permute-start.3) | collective-permute-done | bytes 524320 | tf_op jit(solution)/shard_map/ppermute | solution.py:20
  79.9 16.8 %collective-permute-done.4 = bf16[8,256,128]{2,1,0:T(8,128)(2,1)S(1)} collective-permute-done((bf16[8,256,128]{2,1,0:T(8,128)(2,1)S(1)}, bf16[8,256,128]{2,1,0:T(8,128)(2,1)S(1)}, u32[]{:S(2)}, u32[]{:S(2)}) %collective-permute-start.4) | collective-permute-done | bytes 524320 | tf_op jit(solution)/shard_map/ppermute | solution.py:20
  96.7 13.7 %collective-permute-done.5 = bf16[8,256,128]{2,1,0:T(8,128)(2,1)S(1)} collective-permute-done((bf16[8,256,128]{2,1,0:T(8,128)(2,1)S(1)}, bf16[8,256,128]{2,1,0:T(8,128)(2,1)S(1)}, u32[]{:S(2)}, u32[]{:S(2)}) %collective-permute-start.5) | collective-permute-done | bytes 524320 | tf_op jit(solution)/shard_map/ppermute | solution.py:20
  110.4 27.3 %collective-permute-done.6 = bf16[8,256,128]{2,1,0:T(8,128)(2,1)} collective-permute-done((bf16[8,256,128]{2,1,0:T(8,128)(2,1)S(1)}, bf16[8,256,128]{2,1,0:T(8,128)(2,1)}, u32[]{:S(2)}, u32[]{:S(2)}) %collective-permute-start.6) | collective-permute-done | bytes 524320 | tf_op jit(solution)/shard_map/ppermute | solution.py:20
  138.9 13.0 %collective-permute-done.7 = bf16[8,256,128]{2,1,0:T(8,128)(2,1)} collective-permute-done((bf16[8,256,128]{2,1,0:T(8,128)(2,1)}, bf16[8,256,128]{2,1,0:T(8,128)(2,1)}, u32[]{:S(2)}, u32[]{:S(2)}) %collective-permute-start.7) | collective-permute-done | bytes 524320 | tf_op jit(solution)/shard_map/ppermute | solution.py:20
  155.4 11.3 %collective-permute-done.8 = bf16[8,256,128]{2,1,0:T(8,128)(2,1)} collective-permute-done((bf16[8,256,128]{2,1,0:T(8,128)(2,1)}, bf16[8,256,128]{2,1,0:T(8,128)(2,1)}, u32[]{:S(2)}, u32[]{:S(2)}) %collective-permute-start.8) | collective-permute-done | bytes 524320 | tf_op jit(solution)/shard_map/ppermute | solution.py:20
  168.3 13.4 %collective-permute-done.9 = bf16[8,256,128]{2,1,0:T(8,128)(2,1)S(1)} collective-permute-done((bf16[8,256,128]{2,1,0:T(8,128)(2,1)}, bf16[8,256,128]{2,1,0:T(8,128)(2,1)S(1)}, u32[]{:S(2)}, u32[]{:S(2)}) %collective-permute-start.9) | collective-permute-done | bytes 524320 | tf_op jit(solution)/shard_map/ppermute | solution.py:20
  181.7 8.1 %scatter_custom_fusion = s32[2560]{0:T(1024)S(1)} fusion(s32[2048]{0:T(1024)S(1)} %broadcast_select_fusion.1, s32[2048]{0:T(1024)S(1)} %iota.56, s32[]{:T(128)} %constant.62.clone.1), kind=kCustom, calls=%fused_computation.109 | custom fusion | bytes 10244
  189.8 3.4 fusion.62
  193.3 15.7 %collective-permute-done.10 = bf16[8,256,128]{2,1,0:T(8,128)(2,1)} collective-permute-done((bf16[8,256,128]{2,1,0:T(8,128)(2,1)S(1)}, bf16[8,256,128]{2,1,0:T(8,128)(2,1)}, u32[]{:S(2)}, u32[]{:S(2)}) %collective-permute-start.10) | collective-permute-done | bytes 524320 | tf_op jit(solution)/shard_map/ppermute | solution.py:20
  211.0 13.2 %collective-permute-done.11 = bf16[8,256,128]{2,1,0:T(8,128)(2,1)} collective-permute-done((bf16[8,256,128]{2,1,0:T(8,128)(2,1)}, bf16[8,256,128]{2,1,0:T(8,128)(2,1)}, u32[]{:S(2)}, u32[]{:S(2)}) %collective-permute-start.11) | collective-permute-done | bytes 524320 | tf_op jit(solution)/shard_map/ppermute | solution.py:20
  225.7 14.6 %collective-permute-done.12 = bf16[8,256,128]{2,1,0:T(8,128)(2,1)S(1)} collective-permute-done((bf16[8,256,128]{2,1,0:T(8,128)(2,1)}, bf16[8,256,128]{2,1,0:T(8,128)(2,1)S(1)}, u32[]{:S(2)}, u32[]{:S(2)}) %collective-permute-start.12) | collective-permute-done | bytes 524320 | tf_op jit(solution)/shard_map/ppermute | solution.py:20
  241.2 24.9 %collective-permute-done.13 = bf16[8,256,128]{2,1,0:T(8,128)(2,1)} collective-permute-done((bf16[8,256,128]{2,1,0:T(8,128)(2,1)S(1)}, bf16[8,256,128]{2,1,0:T(8,128)(2,1)}, u32[]{:S(2)}, u32[]{:S(2)}) %collective-permute-start.13) | collective-permute-done | bytes 524320 | tf_op jit(solution)/shard_map/ppermute | solution.py:20
  267.3 22.9 %gather_fusion = bf16[2560,2048]{1,0:T(8,128)(2,1)} fusion(bf16[1024,2048]{1,0:T(8,128)(2,1)} %param.14, s32[3072]{0:T(1024)S(1)} %get-tuple-element.13), kind=kCustom, calls=%fused_computation | custom fusion | bytes 20981760 | tf_op jit(solution)/shard_map/gather | solution.py:96
  341.5 6.7 %fusion.23 = bf16[4,64,512]{2,0,1:T(4,128)(2,1)S(1)} fusion(bf16[64,64,512]{2,1,0:T(8,128)(2,1)} %all-gather.6.cloned.1.call-done, s32[4]{0:T(128)S(1)} %iota_add_fusion.1), kind=kOutput, calls=%fused_computation.31 | convolution fusion | flops 16908544 | bytes 4456464 | tf_op jit(solution)/shard_map/rn,nsc->rsc/dot_general | solution.py:140
  348.4 6.9 %fusion.17 = bf16[4,2048,16]{1,0,2:T(4,128)(2,1)S(1)} fusion(bf16[64,2048,16]{1,2,0:T(8,128)(2,1)} %all-gather.10.cloned.1.call-done, s32[4]{0:T(128)S(1)} %select_reduce_fusion.2), kind=kOutput, calls=%fused_computation.24 | convolution fusion | flops 16908544 | bytes 4456464 | tf_op jit(solution)/shard_map/rn,ndq->rdq/dot_general | solution.py:116
  355.2 3.8 convolution_multiply_fusion
  359.0 6.2 %fusion.20 = bf16[1024,512]{1,0:T(8,128)(2,1)} fusion(f32[4,256,512]{2,1,0:T(8,128)S(1)} %convolution_multiply_fusion, bf16[1024,2048]{1,0:T(8,128)(2,1)} %param.14, bf16[2048,512]{1,0:T(8,128)(2,1)} %all-gather.8.cloned.1.call-done), kind=kOutput, calls=%fused_computation.26 | convolution fusion | flops 2148532224 | bytes 9437184 | tf_op jit(solution)/shard_map/dot_general | solution.py:101
  368.0 9.3 %convolution_convert_fusion = bf16[8,320,256]{2,1,0:T(8,128)(2,1)S(1)} fusion(bf16[8,320,2048]{2,1,0:T(8,128)(2,1)} %bitcast.78, bf16[2048,8,256]{2,0,1:T(8,128)(2,1)} %all-gather.14.cloned.1.call-done), kind=kOutput, calls=%fused_computation.28 | convolution fusion | flops 2685009920 | bytes 20185088 | tf_op jit(solution)/shard_map/kcd,dkh->kch/dot_general | solution.py:102
  377.3 11.1 %gather_fusion.1 = bf16[2048,256]{1,0:T(8,128)(2,1)S(1)} fusion(bf16[8,320,256]{2,1,0:T(8,128)(2,1)S(1)} %convolution_convert_fusion, s32[2048]{0:T(1024)S(1)} %bitcast.75), kind=kCustom, calls=%fused_computation.1 | custom fusion | bytes 2113536 | tf_op jit(solution)/shard_map/gather | solution.py:147
  388.8 6.3 %fusion.57 = (f32[4,2,256,2]{2,3,1,0:T(2,128)S(1)}, f32[4,2,256,2,320]{2,4,3,1,0:T(8,128)}) fusion(pred[4,256,320]{1,2,0:T(8,128)(4,1)S(1)} %copy-done.11, bf16[4,256,2,2,128]{4,3,2,1,0:T(2,128)(2,1)S(1)} %reshape.178, bf16[4,320,2,2,128]{4,1,2,0,3:T(8,128)(2,1)} %copy-done.12), kind=kOutput, calls=%fused_computation.131 | convolution fusion | flops 678953280 | bytes 9322496 | tf_op jit(solution)/shard_map/sub | solution.py:60
  395.0 3.3 fusion.22
  399.2 7.6 %gather_fusion.2 = bf16[2560,256]{1,0:T(8,128)(2,1)S(1)} fusion(bf16[2048,256]{1,0:T(8,128)(2,1)S(1)} %bitcast.77, s32[3072]{0:T(1024)S(1)} %get-tuple-element.12), kind=kCustom, calls=%fused_computation.2 | custom fusion | bytes 2631680 | tf_op jit(solution)/shard_map/gather | solution.py:151
  406.8 12.2 %fusion.1 = f32[8,320,2048]{2,1,0:T(8,128)} fusion(bf16[8,320,256]{2,1,0:T(8,128)(2,1)S(1)} %bitcast.79, bf16[8,256,4096]{2,1,0:T(8,128)(2,1)} %constant_dynamic-update-slice_fusion, s32[]{:T(128)S(6)} %select_n.76), kind=kOutput, calls=%fused_computation.8 | convolution fusion | flops 2684354560 | bytes 30670852 | tf_op jit(solution)/shard_map/kch,khn->kcn/dot_general | solution.py:164
  419.0 51.1 %gather_fusion.3 = f32[2048,2048]{1,0:T(8,128)} fusion(f32[8,320,2048]{2,1,0:T(8,128)} %fusion.1, s32[2048]{0:T(1024)S(1)} %bitcast.76), kind=kCustom, calls=%fused_computation.3 | custom fusion | bytes 33570816 | tf_op jit(solution)/shard_map/gather | solution.py:167
  470.1 20.0 %reshape.180 = f32[1024,2,2048]{2,1,0:T(2,128)} reshape(f32[2048,2048]{1,0:T(8,128)} %gather_fusion.3) | data formatting | bytes 33554432 | tf_op jit(solution)/shard_map/reshape | solution.py:167
  490.1 30.3 %multiply_reduce_fusion = f32[1024,2048]{1,0:T(8,128)} fusion(f32[1024,2,2048]{2,1,0:T(2,128)} %reshape.180, f32[1024,2]{1,0:T(8,128)S(1)} %copy.61), kind=kLoop, calls=%fused_computation.6 | loop fusion | flops 6291456 | bytes 25174016 | tf_op jit(solution)/shard_map/reduce_sum | solution.py:168
  520.4 5.8 %multiply_convert_fusion = bf16[1024,2048]{1,0:T(8,128)(2,1)} fusion(f32[1024,2048]{1,0:T(8,128)} %multiply_reduce_fusion, f32[1024]{0:T(1024)S(1)} %bitcast.82), kind=kLoop, calls=%fused_computation.7 | loop fusion | flops 4194304 | bytes 12587008 | tf_op jit(solution)/shard_map/convert_element_type | solution.py:170
  526.3 39.1 %reduce-scatter.2.cloned.1.call-done = bf16[1024,256]{1,0:T(8,128)(2,1)} async-done(((bf16[1024,2048]{1,0:T(8,128)(2,1)}), bf16[1024,256]{1,0:T(8,128)(2,1)}) %reduce-scatter.2.cloned.1.call-update) | async-done | bytes 524304 | tf_op jit(solution)/shard_map/reduce_scatter | solution.py:169
  (136 shorter events, 74.2 us)
Async XLA Ops:
  6.5 183.3 %copy-start = (bf16[2048,8]{0,1:T(8,128)(2,1)S(1)}, bf16[2048,8]{0,1:T(8,128)(2,1)}, u32[]{:S(2)}) copy-start(bf16[2048,8]{0,1:T(8,128)(2,1)} %param.21) | copy-start | bytes 98308
  6.5 284.9 %all-gather.12.cloned.1.call-start = ((), (), s32[]{:S(2)}) async-start(), calls=%async_computation.4 | async-start | bytes 1114112 | tf_op jit(solution)/shard_map/all_gather | solution.py:110
  7.3 334.3 %all-gather.6.cloned.1.call-start = ((), (), s32[]{:S(2)}) async-start(), calls=%async_computation.1 | async-start | bytes 4456448 | tf_op jit(solution)/shard_map/all_gather | solution.py:135
  8.0 340.3 %all-gather.10.cloned.1.call-start = ((), (), s32[]{:S(2)}) async-start(), calls=%async_computation.3 | async-start | bytes 4456448 | tf_op jit(solution)/shard_map/all_gather | solution.py:109
  8.7 350.3 %all-gather.8.cloned.1.call-start = ((), (), s32[]{:S(2)}) async-start(), calls=%async_computation.2 | async-start | bytes 2228224 | tf_op jit(solution)/shard_map/all_gather | solution.py:98
  9.3 357.7 %all-gather.14.cloned.1.call-start = ((), (), s32[]{:S(2)}) async-start(), calls=%async_computation.5 | async-start | bytes 8912896 | tf_op jit(solution)/shard_map/all_gather | solution.py:99
  11.3 554.1 %reduce-scatter.2.cloned.1.call-start = ((), (), s32[]{:S(2)}) async-start(), calls=%async_computation.6 | async-start | bytes 4718592 | tf_op jit(solution)/shard_map/reduce_scatter | solution.py:169
  11.4 18.9 %collective-permute-start = (bf16[8,256,128]{2,1,0:T(8,128)(2,1)}, bf16[8,256,128]{2,1,0:T(8,128)(2,1)S(1)}, u32[]{:S(2)}, u32[]{:S(2)}) collective-permute-start(bf16[8,256,128]{2,1,0:T(8,128)(2,1)} %param.24), channel_id=1, source_target_pairs={{0,8},{8,16},{16,24},{24,32},{32,40},{40,48},{48,56},{56,64},{64,7... | collective-permute-start | bytes 1572872 | tf_op jit(solution)/shard_map/ppermute | solution.py:20
  30.3 16.5 %collective-permute-start.1 = (bf16[8,256,128]{2,1,0:T(8,128)(2,1)S(1)}, bf16[8,256,128]{2,1,0:T(8,128)(2,1)S(1)}, u32[]{:S(2)}, u32[]{:S(2)}) collective-permute-start(bf16[8,256,128]{2,1,0:T(8,128)(2,1)S(1)} %collective-permute-done), channel_id=1, source_target_pairs={{0,8},{8,16},{16,24},{24,32},{32,40},{40,48},{48,56},{56,64},{64,7... | collective-permute-start | bytes 1572872 | tf_op jit(solution)/shard_map/ppermute | solution.py:20
  46.8 19.6 %collective-permute-start.2 = (bf16[8,256,128]{2,1,0:T(8,128)(2,1)S(1)}, bf16[8,256,128]{2,1,0:T(8,128)(2,1)S(1)}, u32[]{:S(2)}, u32[]{:S(2)}) collective-permute-start(bf16[8,256,128]{2,1,0:T(8,128)(2,1)S(1)} %collective-permute-done.1), channel_id=1, source_target_pairs={{0,8},{8,16},{16,24},{24,32},{32,40},{40,48},{48,56},{56,64},{64,7... | collective-permute-start | bytes 1572872 | tf_op jit(solution)/shard_map/ppermute | solution.py:20
  66.4 13.5 %collective-permute-start.3 = (bf16[8,256,128]{2,1,0:T(8,128)(2,1)S(1)}, bf16[8,256,128]{2,1,0:T(8,128)(2,1)S(1)}, u32[]{:S(2)}, u32[]{:S(2)}) collective-permute-start(bf16[8,256,128]{2,1,0:T(8,128)(2,1)S(1)} %collective-permute-done.2), channel_id=1, source_target_pairs={{0,8},{8,16},{16,24},{24,32},{32,40},{40,48},{48,56},{56,64},{64,7... | collective-permute-start | bytes 1572872 | tf_op jit(solution)/shard_map/ppermute | solution.py:20
  79.9 16.8 %collective-permute-start.4 = (bf16[8,256,128]{2,1,0:T(8,128)(2,1)S(1)}, bf16[8,256,128]{2,1,0:T(8,128)(2,1)S(1)}, u32[]{:S(2)}, u32[]{:S(2)}) collective-permute-start(bf16[8,256,128]{2,1,0:T(8,128)(2,1)S(1)} %collective-permute-done.3), channel_id=1, source_target_pairs={{0,8},{8,16},{16,24},{24,32},{32,40},{40,48},{48,56},{56,64},{64,7... | collective-permute-start | bytes 1572872 | tf_op jit(solution)/shard_map/ppermute | solution.py:20
  96.7 193.5 %copy-start.3 = (bf16[8,256,128]{2,1,0:T(8,128)(2,1)}, bf16[8,256,128]{2,1,0:T(8,128)(2,1)S(1)}, u32[]{:S(2)}) copy-start(bf16[8,256,128]{2,1,0:T(8,128)(2,1)S(1)} %collective-permute-done.4) | copy-start | bytes 1572868
  96.7 13.7 %collective-permute-start.5 = (bf16[8,256,128]{2,1,0:T(8,128)(2,1)S(1)}, bf16[8,256,128]{2,1,0:T(8,128)(2,1)S(1)}, u32[]{:S(2)}, u32[]{:S(2)}) collective-permute-start(bf16[8,256,128]{2,1,0:T(8,128)(2,1)S(1)} %collective-permute-done.4), channel_id=1, source_target_pairs={{0,8},{8,16},{16,24},{24,32},{32,40},{40,48},{48,56},{56,64},{64,7... | collective-permute-start | bytes 1572872 | tf_op jit(solution)/shard_map/ppermute | solution.py:20
  110.4 27.3 %copy-start.5 = (bf16[8,256,128]{2,1,0:T(8,128)(2,1)}, bf16[8,256,128]{2,1,0:T(8,128)(2,1)S(1)}, u32[]{:S(2)}) copy-start(bf16[8,256,128]{2,1,0:T(8,128)(2,1)S(1)} %collective-permute-done.5) | copy-start | bytes 1572868
  110.4 27.3 %collective-permute-start.6 = (bf16[8,256,128]{2,1,0:T(8,128)(2,1)S(1)}, bf16[8,256,128]{2,1,0:T(8,128)(2,1)}, u32[]{:S(2)}, u32[]{:S(2)}) collective-permute-start(bf16[8,256,128]{2,1,0:T(8,128)(2,1)S(1)} %collective-permute-done.5), channel_id=1, source_target_pairs={{0,8},{8,16},{16,24},{24,32},{32,40},{40,48},{48,56},{56,64},{64,7... | collective-permute-start | bytes 1572872 | tf_op jit(solution)/shard_map/ppermute | solution.py:20
  137.7 14.2 %collective-permute-start.7 = (bf16[8,256,128]{2,1,0:T(8,128)(2,1)}, bf16[8,256,128]{2,1,0:T(8,128)(2,1)}, u32[]{:S(2)}, u32[]{:S(2)}) collective-permute-start(bf16[8,256,128]{2,1,0:T(8,128)(2,1)} %collective-permute-done.6), channel_id=1, source_target_pairs={{0,8},{8,16},{16,24},{24,32},{32,40},{40,48},{48,56},{56,64},{64,7... | collective-permute-start | bytes 1572872 | tf_op jit(solution)/shard_map/ppermute | solution.py:20
  151.9 14.8 %collective-permute-start.8 = (bf16[8,256,128]{2,1,0:T(8,128)(2,1)}, bf16[8,256,128]{2,1,0:T(8,128)(2,1)}, u32[]{:S(2)}, u32[]{:S(2)}) collective-permute-start(bf16[8,256,128]{2,1,0:T(8,128)(2,1)} %collective-permute-done.7), channel_id=1, source_target_pairs={{0,8},{8,16},{16,24},{24,32},{32,40},{40,48},{48,56},{56,64},{64,7... | collective-permute-start | bytes 1572872 | tf_op jit(solution)/shard_map/ppermute | solution.py:20
  166.7 14.9 %collective-permute-start.9 = (bf16[8,256,128]{2,1,0:T(8,128)(2,1)}, bf16[8,256,128]{2,1,0:T(8,128)(2,1)S(1)}, u32[]{:S(2)}, u32[]{:S(2)}) collective-permute-start(bf16[8,256,128]{2,1,0:T(8,128)(2,1)} %collective-permute-done.8), channel_id=1, source_target_pairs={{0,8},{8,16},{16,24},{24,32},{32,40},{40,48},{48,56},{56,64},{64,7... | collective-permute-start | bytes 1572872 | tf_op jit(solution)/shard_map/ppermute | solution.py:20
  181.7 85.6 %copy-start.7 = (bf16[8,256,128]{2,1,0:T(8,128)(2,1)}, bf16[8,256,128]{2,1,0:T(8,128)(2,1)S(1)}, u32[]{:S(2)}) copy-start(bf16[8,256,128]{2,1,0:T(8,128)(2,1)S(1)} %collective-permute-done.9) | copy-start | bytes 1572868
  181.7 27.3 %collective-permute-start.10 = (bf16[8,256,128]{2,1,0:T(8,128)(2,1)S(1)}, bf16[8,256,128]{2,1,0:T(8,128)(2,1)}, u32[]{:S(2)}, u32[]{:S(2)}) collective-permute-start(bf16[8,256,128]{2,1,0:T(8,128)(2,1)S(1)} %collective-permute-done.9), channel_id=1, source_target_pairs={{0,8},{8,16},{16,24},{24,32},{32,40},{40,48},{48,56},{56,64},{64,7... | collective-permute-start | bytes 1572872 | tf_op jit(solution)/shard_map/ppermute | solution.py:20
  209.0 15.2 %collective-permute-start.11 = (bf16[8,256,128]{2,1,0:T(8,128)(2,1)}, bf16[8,256,128]{2,1,0:T(8,128)(2,1)}, u32[]{:S(2)}, u32[]{:S(2)}) collective-permute-start(bf16[8,256,128]{2,1,0:T(8,128)(2,1)} %collective-permute-done.10), channel_id=1, source_target_pairs={{0,8},{8,16},{16,24},{24,32},{32,40},{40,48},{48,56},{56,64},{64,7... | collective-permute-start | bytes 1572872 | tf_op jit(solution)/shard_map/ppermute | solution.py:20
  224.2 16.0 %collective-permute-start.12 = (bf16[8,256,128]{2,1,0:T(8,128)(2,1)}, bf16[8,256,128]{2,1,0:T(8,128)(2,1)S(1)}, u32[]{:S(2)}, u32[]{:S(2)}) collective-permute-start(bf16[8,256,128]{2,1,0:T(8,128)(2,1)} %collective-permute-done.11), channel_id=1, source_target_pairs={{0,8},{8,16},{16,24},{24,32},{32,40},{40,48},{48,56},{56,64},{64,7... | collective-permute-start | bytes 1572872 | tf_op jit(solution)/shard_map/ppermute | solution.py:20
  241.0 25.1 %collective-permute-start.13 = (bf16[8,256,128]{2,1,0:T(8,128)(2,1)S(1)}, bf16[8,256,128]{2,1,0:T(8,128)(2,1)}, u32[]{:S(2)}, u32[]{:S(2)}) collective-permute-start(bf16[8,256,128]{2,1,0:T(8,128)(2,1)S(1)} %collective-permute-done.12), channel_id=1, source_target_pairs={{0,8},{8,16},{16,24},{24,32},{32,40},{40,48},{48,56},{56,64},{64,7... | collective-permute-start | bytes 1572872 | tf_op jit(solution)/shard_map/ppermute | solution.py:20
  266.1 27.9 %collective-permute-start.14 = (bf16[8,256,128]{2,1,0:T(8,128)(2,1)}, bf16[8,256,128]{2,1,0:T(8,128)(2,1)}, u32[]{:S(2)}, u32[]{:S(2)}) collective-permute-start(bf16[8,256,128]{2,1,0:T(8,128)(2,1)} %collective-permute-done.13), channel_id=1, source_target_pairs={{0,8},{8,16},{16,24},{24,32},{32,40},{40,48},{48,56},{56,64},{64,7... | collective-permute-start | bytes 1572872 | tf_op jit(solution)/shard_map/ppermute | solution.py:20
  290.2 28.7 %copy-start.2 = (bf16[8,256,128]{2,1,0:T(8,128)(2,1)S(1)}, bf16[8,256,128]{2,1,0:T(8,128)(2,1)}, u32[]{:S(2)}) copy-start(bf16[8,256,128]{2,1,0:T(8,128)(2,1)} %param.24) | copy-start | bytes 1572868
  291.4 32.2 %copy-start.10 = (bf16[8,256,128]{2,1,0:T(8,128)(2,1)S(1)}, bf16[8,256,128]{2,1,0:T(8,128)(2,1)}, u32[]{:S(2)}) copy-start(bf16[8,256,128]{2,1,0:T(8,128)(2,1)} %copy-done.9) | copy-start | bytes 1572868
  291.4 37.1 %copy-start.8 = (bf16[8,256,128]{2,1,0:T(8,128)(2,1)S(1)}, bf16[8,256,128]{2,1,0:T(8,128)(2,1)}, u32[]{:S(2)}) copy-start(bf16[8,256,128]{2,1,0:T(8,128)(2,1)} %copy-done.7) | copy-start | bytes 1572868
  291.4 43.8 %copy-start.6 = (bf16[8,256,128]{2,1,0:T(8,128)(2,1)S(1)}, bf16[8,256,128]{2,1,0:T(8,128)(2,1)}, u32[]{:S(2)}) copy-start(bf16[8,256,128]{2,1,0:T(8,128)(2,1)} %copy-done.5) | copy-start | bytes 1572868
  291.4 44.7 %copy-start.4 = (bf16[8,256,128]{2,1,0:T(8,128)(2,1)S(1)}, bf16[8,256,128]{2,1,0:T(8,128)(2,1)}, u32[]{:S(2)}) copy-start(bf16[8,256,128]{2,1,0:T(8,128)(2,1)} %copy-done.3) | copy-start | bytes 1572868
  368.0 20.7 %copy-start.11 = (pred[4,256,320]{1,2,0:T(8,128)(4,1)S(1)}, pred[4,256,320]{1,2,0:T(8,128)(4,1)}, u32[]{:S(2)}) copy-start(pred[4,256,320]{1,2,0:T(8,128)(4,1)} %broadcast_select_fusion) | copy-start | bytes 983044
  470.1 95.3 %copy-start.1 = (bf16[2048,8]{0,1:T(8,128)(2,1)S(1)}, bf16[2048,8]{0,1:T(8,128)(2,1)}, u32[]{:S(2)}) copy-start(bf16[2048,8]{0,1:T(8,128)(2,1)} %param.21) | copy-start | bytes 98308
  (3 other events, 8.1 us)
Sparse Core Ops, SparseCore 0:
  9.5 57.5 all-gather.11
  69.3 69.1 all-gather.5
  140.7 71.2 all-gather.9
  213.9 46.2 all-gather.7
  262.3 74.5 all-gather.13
  526.4 38.9 reduce-scatter.1
